TPU v7x, 32 devices: a whole 2x2x4 slice. The times are simulated.
32 devices in a mesh: frames: 8 (over z, x), mp: 4 (over y, core).
Axes of the slice: x: 2, y: 2, z: 4, core: 2. Of those that a mesh axis runs over, the one named last changes fastest.
Arguments:
- features: bfloat16 [1024, 512], P('frames'), may hold values from -32 to 32
- logit_weight: bfloat16 [512, 640], replicated, may hold values from -1 to 1
- gumbel_perturbation: float32 [1024, 640], P('frames'), may hold values from -3 to 12
- codebook: bfloat16 [640, 384], replicated, may hold values from -6 to 6
- project_weight: bfloat16 [768, 768], P(None, 'mp'), may hold values from -0.21875 to 0.21875
- context: bfloat16 [1024, 768], P('frames', 'mp'), may hold values from -6 to 6
- distractors: int32 [1024, 100], P('frames'), may hold values from 0 to 1023, as said below
- masked: int32 [1024], P('frames'), may hold values from 0 to 1
Outputs:
- scores: float32 [1024, 101], P('frames')
- loss: float32 [], replicated
- diversity: float32 [], replicated
Inputs may be any that keep to these rules, and one draw needn't show every extreme that they name: `distractors`: the distractor of a frame in shard s (frames s * 128 to s * 128 + 127) lies in shard s + o modulo 1024 // 128, with 1 <= |o| <= 3.
All inputs are finite; a program needn't handle non-finite values.
Results may differ from a plain program's by a relative error of at most 0.0049.
Values may be sent and summed in bfloat16 or wider, within the bound.
A program may use at most 64 MiB of HBM per device.

v0:
```python
import jax
import jax.numpy as jnp
from jax import lax
from jax.sharding import PartitionSpec as P

V = 320
G = 2
REACH = 3


gumbel_softness = 2.0
logit_softness = 0.1
norm_epsilon = 1e-06


def from_behind(value, axis, steps):
    count = lax.axis_size(axis)
    pairs = [(source, (source + steps) % count) for source in range(count)]
    return lax.ppermute(value, axis, pairs)


def grouped_softmax(values):
    count = values.shape[0]
    shaped = values.reshape(count, G, -1)
    top = jnp.max(shaped, axis=2, keepdims=True)
    expd = jnp.exp(shaped - top)
    return (expd / jnp.sum(expd, axis=2, keepdims=True)).reshape(count, -1)


def select_columns(sims, slot, local_row, count, slots_all):
    block_rows = max(count // 16, 1)
    blocks = count // block_rows
    sims_blocks = sims.reshape(blocks, block_rows, slots_all, count)
    slot_blocks = slot.reshape(blocks, block_rows, -1)
    row_blocks = local_row.reshape(blocks, block_rows, -1)
    columns = jnp.arange(count, dtype=jnp.int32)

    def one_block(triple):
        sims_part, slot_part, row_part = triple
        hits = row_part[:, :, None] == columns[None, None, :]
        picked = jnp.zeros(slot_part.shape, jnp.float32)
        for which in range(slots_all):
            values = jnp.sum(
                jnp.where(hits, sims_part[:, which, None, :], jnp.float32(0.0)), axis=2
            )
            picked = picked + jnp.where(slot_part == which, values, jnp.float32(0.0))
        return picked

    return lax.map(one_block, (sims_blocks, slot_blocks, row_blocks)).reshape(count, -1)


def on_device(
    features,
    logit_weight,
    gumbel_perturbation,
    codebook,
    project_weight,
    context,
    distractors,
    masked,
):
    count = features.shape[0]
    shards = lax.axis_size("frames")
    own = lax.axis_index("frames")
    codeword_logits = jnp.dot(features, logit_weight, preferred_element_type=jnp.float32)
    clean = grouped_softmax(codeword_logits)
    prob_total = jnp.sum(clean, axis=0)
    prob_total = lax.psum(prob_total, "frames")
    soft_assignment = grouped_softmax(
        (codeword_logits + gumbel_perturbation) / gumbel_softness
    ).astype(jnp.bfloat16)
    pieces = [
        jnp.dot(
            soft_assignment[:, g * V : (g + 1) * V],
            codebook[g * V : (g + 1) * V],
            preferred_element_type=jnp.float32,
        )
        for g in range(G)
    ]
    codevec = jnp.concatenate(pieces, axis=1).astype(jnp.bfloat16)
    target = jnp.dot(codevec, project_weight, preferred_element_type=jnp.float32)
    norm_sq = lax.psum(jnp.sum(target * target, axis=1), "mp")
    unit = (target * lax.rsqrt(norm_sq + norm_epsilon)[:, None]).astype(jnp.bfloat16)
    owner = distractors // count
    local_row = distractors - owner * count
    distance = (owner - own + shards) % shards
    slot = jnp.where(distance <= REACH, (distance - 1) * 2, (shards - distance - 1) * 2 + 1)
    fetched = []
    for offset in range(1, REACH + 1):
        for sign in (1, -1):
            fetched.append(from_behind(unit, "frames", -sign * offset))
    stacked = jnp.concatenate(fetched, axis=0)
    sims = jnp.einsum("tf,sf->ts", context, stacked, preferred_element_type=jnp.float32)
    other_dot = select_columns(sims, slot, local_row, count, 2 * REACH)
    ctx_float = context.astype(jnp.float32)
    ctx_part = jnp.sum(ctx_float * ctx_float, axis=1)
    self_dot = jnp.sum(ctx_float * unit.astype(jnp.float32), axis=1)
    inner_products = jnp.concatenate([self_dot[:, None], other_dot], axis=1)
    inner_products, context_squared = lax.psum((inner_products, ctx_part), "mp")
    scores = inner_products * lax.rsqrt(context_squared + norm_epsilon)[:, None] / logit_softness
    cross = jnp.log(jnp.sum(jnp.exp(scores), axis=1)) - scores[:, 0]
    loss_part = jnp.sum(jnp.where(masked == 1, cross, jnp.float32(0.0)))
    loss_total = lax.psum(loss_part, "frames")
    frames_all = count * shards
    loss = loss_total / frames_all
    usage = (prob_total / frames_all).reshape(G, V)
    perplex = jnp.sum(jnp.exp(-jnp.sum(usage * jnp.log(usage + 1e-07), axis=1)))
    diversity = (G * V - perplex) / (G * V)
    return (scores, loss, diversity)


def solution(mesh):
    return jax.shard_map(
        on_device,
        mesh=mesh,
        in_specs=(
            P("frames", None),
            P(),
            P("frames", None),
            P(),
            P(None, "mp"),
            P("frames", "mp"),
            P("frames", None),
            P("frames"),
        ),
        out_specs=(P("frames", None), P(), P()),
        check_vma=False,
    )
```

profile of v0, /device:TPU:0, one launch (start us, length us, event | category | flops | bytes accessed | tf_op | source)
XLA Modules:
  0.0 91.2 jit_solution(6944786442795773589)
XLA Ops:
  0.6 1.1 %copy-done = bf16[512,640]{1,0:T(8,128)(2,1)S(1)} copy-done((bf16[512,640]{1,0:T(8,128)(2,1)S(1)}, bf16[512,640]{1,0:T(8,128)(2,1)}, u32[]{:S(2)}) %copy-start) | copy-done | bytes 655384
  1.7 1.2 %fusion.43 = f32[128,640]{1,0:T(8,128)S(1)} fusion(bf16[128,512]{1,0:T(8,128)(2,1)} %param.10, bf16[512,640]{1,0:T(8,128)(2,1)S(1)} %copy-done), kind=kOutput, calls=%fused_computation.97 | convolution fusion | flops 83886080 | bytes 1114112 | tf_op jit(solution)/shard_map/dot_general | solution.py:65
  2.9 0.2 copy.62
  3.1 0.2 fusion.19
  3.5 0.2 copy.63
  3.7 0.8 copy-done.1
  4.8 0.2 fusion.20
  5.0 0.2 copy.51
  5.5 0.9 %copy-done.5 = bf16[640,384]{1,0:T(8,128)(2,1)S(1)} copy-done((bf16[640,384]{1,0:T(8,128)(2,1)S(1)}, bf16[640,384]{1,0:T(8,128)(2,1)}, u32[]{:S(2)}) %copy-start.5) | copy-done | bytes 491544
  6.4 0.3 convolution_convert_fusion
  6.7 0.2 convolution_convert_fusion.1
  6.9 0.7 copy-done.6
  7.6 0.3 multiply_reduce_fusion
  7.9 8.4 %psum.35 = f32[128]{0:T(128)S(1)} all-reduce(f32[128]{0:T(128)S(1)} %get-tuple-element.117), channel_id=1, replica_groups=mesh['frames'=8,'mp'=4] {'mp'}, use_global_device_ids=true, to_apply=%region_3.0 | all-reduce | flops 128 | bytes 1024 | tf_op jit(solution)/shard_map/psum | solution.py:82
  16.4 4.6 %collective-permute-start = (bf16[128,192]{0,1:T(8,128)(2,1)S(1)}, bf16[128,192]{0,1:T(8,128)(2,1)S(1)}, u32[]{:S(2)}, u32[]{:S(2)}) collective-permute-start(bf16[128,192]{0,1:T(8,128)(2,1)S(1)} %get-tuple-element.104), channel_id=1, source_target_pairs={{0,28},{4,0},{8,4},{12,8},{16,12},{20,16},{24,20},{28,24},{1,29},{... | collective-permute-start | bytes 147464 | tf_op jit(solution)/shard_map/ppermute | solution.py:19
  20.9 1.1 %collective-permute-start.2 = (bf16[128,192]{0,1:T(8,128)(2,1)S(1)}, bf16[128,192]{0,1:T(8,128)(2,1)S(1)}, u32[]{:S(2)}, u32[]{:S(2)}) collective-permute-start(bf16[128,192]{0,1:T(8,128)(2,1)S(1)} %get-tuple-element.104), channel_id=1, source_target_pairs={{0,24},{4,28},{8,0},{12,4},{16,8},{20,12},{24,16},{28,20},{1,25},{... | collective-permute-start | bytes 147464 | tf_op jit(solution)/shard_map/ppermute | solution.py:19
  22.0 0.9 %collective-permute-start.3 = (bf16[128,192]{0,1:T(8,128)(2,1)S(1)}, bf16[128,192]{0,1:T(8,128)(2,1)S(1)}, u32[]{:S(2)}, u32[]{:S(2)}) collective-permute-start(bf16[128,192]{0,1:T(8,128)(2,1)S(1)} %get-tuple-element.104), channel_id=1, source_target_pairs={{0,8},{4,12},{8,16},{12,20},{16,24},{20,28},{24,0},{28,4},{1,9},{5... | collective-permute-start | bytes 147464 | tf_op jit(solution)/shard_map/ppermute | solution.py:19
  23.0 3.3 %collective-permute-start.4 = (bf16[128,192]{0,1:T(8,128)(2,1)S(1)}, bf16[128,192]{0,1:T(8,128)(2,1)S(1)}, u32[]{:S(2)}, u32[]{:S(2)}) collective-permute-start(bf16[128,192]{0,1:T(8,128)(2,1)S(1)} %get-tuple-element.104), channel_id=1, source_target_pairs={{0,20},{4,24},{8,28},{12,0},{16,4},{20,8},{24,12},{28,16},{1,21},{... | collective-permute-start | bytes 147464 | tf_op jit(solution)/shard_map/ppermute | solution.py:19
  26.6 1.1 %collective-permute-done.1 = bf16[128,192]{0,1:T(8,128)(2,1)S(1)} collective-permute-done((bf16[128,192]{0,1:T(8,128)(2,1)S(1)}, bf16[128,192]{0,1:T(8,128)(2,1)S(1)}, u32[]{:S(2)}, u32[]{:S(2)}) %collective-permute-start.1) | collective-permute-done | bytes 49184 | tf_op jit(solution)/shard_map/ppermute | solution.py:19
  27.8 0.2 collective-permute-done.3
  28.0 0.8 collective-permute-done.4
  28.8 4.0 %collective-permute-done.5 = bf16[128,192]{0,1:T(8,128)(2,1)S(1)} collective-permute-done((bf16[128,192]{0,1:T(8,128)(2,1)S(1)}, bf16[128,192]{0,1:T(8,128)(2,1)S(1)}, u32[]{:S(2)}, u32[]{:S(2)}) %collective-permute-start.5) | collective-permute-done | bytes 49184 | tf_op jit(solution)/shard_map/ppermute | solution.py:19
  32.8 0.3 convolution_bitcast_fusion
  33.1 0.2 copy.57
  33.3 19.4 %while.11 = (s32[]{:T(128)}, f32[16,8,100]{2,1,0:T(8,128)S(1)}, s32[16,8,100]{2,1,0:T(8,128)S(1)}, s32[16,8,100]{2,1,0:T(8,128)S(1)}, f32[16,8,6,128]{3,1,2,0:T(8,128)S(1)}, /*index=5*/s32[]{:T(128)}) while((s32[]{:T(128)}, f32[16,8,100]{2,1,0:T(8,128)S(1)}, s32[16,8,100]{2,1,0:T(8,128)S(1)}, s32[16,8,100]{2,1,0:T(8,128)S(1)}, ...), condition=%wide.region_12.13_spmd.clone, body=%wide.region_5.12_spmd.clone.sunk | while | flops 1340002 | bytes 211153 | solution.py:49
  33.4 0.8 fusion.51
  34.7 0.8 fusion.51
  35.9 0.8 fusion.51
  37.1 0.8 fusion.51
  38.3 0.8 fusion.51
  39.5 0.8 fusion.51
  40.7 0.8 fusion.51
  41.9 0.8 fusion.51
  43.1 0.8 fusion.51
  44.4 0.8 fusion.51
  45.6 0.8 fusion.51
  46.8 0.8 fusion.51
  48.0 0.8 fusion.51
  49.2 0.8 fusion.51
  50.4 0.8 fusion.51
  51.6 0.8 fusion.51
  52.8 11.0 %all-reduce.1 = (f32[128,101]{1,0:T(8,128)S(1)}, f32[128]{0:T(128)S(1)}) all-reduce(f32[128,101]{1,0:T(8,128)S(1)} %pad_maximum_fusion, f32[128]{0:T(128)S(1)} %get-tuple-element.86), channel_id=1, replica_groups=mesh['frames'=8,'mp'=4] {'mp'}, use_global_device_ids=true, to_apply=%region_13.14 | all-reduce | flops 13056 | bytes 104448 | tf_op jit(solution)/shard_map/psum | solution.py:99
  63.8 0.2 exponential_reduce_fusion.2
  64.1 0.7 copy.65
  64.8 0.7 copy-done.4
  65.5 0.6 fusion.41
  66.1 20.8 %all-reduce = (f32[]{:T(128)}, f32[640]{0:T(1024)S(1)}) all-reduce(f32[]{:T(128)} %fusion.41, f32[640]{0:T(1024)S(1)} %get-tuple-element.113), channel_id=1, replica_groups=mesh['frames'=8,'mp'=4] {'frames'}, use_global_device_ids=true, to_apply=%region_18.19 | all-reduce | flops 641 | bytes 5128 | tf_op jit(solution)/shard_map/psum | solution.py:103
  87.1 0.6 exponential_reduce_fusion.3
  (168 shorter events, 7.3 us)
Async XLA Ops:
  0.6 1.1 %copy-start = (bf16[512,640]{1,0:T(8,128)(2,1)S(1)}, bf16[512,640]{1,0:T(8,128)(2,1)}, u32[]{:S(2)}) copy-start(bf16[512,640]{1,0:T(8,128)(2,1)} %param.11) | copy-start | bytes 1966084
  3.5 1.0 %copy-start.1 = (f32[128,640]{1,0:T(8,128)S(1)}, f32[128,640]{1,0:T(8,128)}, u32[]{:S(2)}) copy-start(f32[128,640]{1,0:T(8,128)} %param.12) | copy-start | bytes 983044
  5.4 1.0 %copy-start.5 = (bf16[640,384]{1,0:T(8,128)(2,1)S(1)}, bf16[640,384]{1,0:T(8,128)(2,1)}, u32[]{:S(2)}) copy-start(bf16[640,384]{1,0:T(8,128)(2,1)} %param.13) | copy-start | bytes 1474564
  6.7 1.0 %copy-start.6 = (bf16[768,192]{0,1:T(8,128)(2,1)S(1)}, bf16[768,192]{0,1:T(8,128)(2,1)}, u32[]{:S(2)}) copy-start(bf16[768,192]{0,1:T(8,128)(2,1)} %param.14) | copy-start | bytes 884740
  7.6 8.7 %copy-start.2 = (bf16[128,192]{0,1:T(8,128)(2,1)S(1)}, bf16[128,192]{0,1:T(8,128)(2,1)}, u32[]{:S(2)}) copy-start(bf16[128,192]{0,1:T(8,128)(2,1)} %param.15) | copy-start | bytes 147460
  16.3 9.9 %copy-start.3 = (s32[128,100]{0,1:T(8,128)S(1)}, s32[128,100]{0,1:T(8,128)}, u32[]{:S(2)}) copy-start(s32[128,100]{0,1:T(8,128)} %param.16) | copy-start | bytes 153604
  16.4 10.2 %collective-permute-start = (bf16[128,192]{0,1:T(8,128)(2,1)S(1)}, bf16[128,192]{0,1:T(8,128)(2,1)S(1)}, u32[]{:S(2)}, u32[]{:S(2)}) collective-permute-start(bf16[128,192]{0,1:T(8,128)(2,1)S(1)} %get-tuple-element.104), channel_id=1, source_target_pairs={{0,28},{4,0},{8,4},{12,8},{16,12},{20,16},{24,20},{28,24},{1,29},{... | collective-permute-start | bytes 147464 | tf_op jit(solution)/shard_map/ppermute | solution.py:19
  20.9 6.8 %collective-permute-start.1 = (bf16[128,192]{0,1:T(8,128)(2,1)S(1)}, bf16[128,192]{0,1:T(8,128)(2,1)S(1)}, u32[]{:S(2)}, u32[]{:S(2)}) collective-permute-start(bf16[128,192]{0,1:T(8,128)(2,1)S(1)} %get-tuple-element.104), channel_id=1, source_target_pairs={{0,4},{4,8},{8,12},{12,16},{16,20},{20,24},{24,28},{28,0},{1,5},{5... | collective-permute-start | bytes 147464 | tf_op jit(solution)/shard_map/ppermute | solution.py:19
  20.9 6.8 %collective-permute-start.2 = (bf16[128,192]{0,1:T(8,128)(2,1)S(1)}, bf16[128,192]{0,1:T(8,128)(2,1)S(1)}, u32[]{:S(2)}, u32[]{:S(2)}) collective-permute-start(bf16[128,192]{0,1:T(8,128)(2,1)S(1)} %get-tuple-element.104), channel_id=1, source_target_pairs={{0,24},{4,28},{8,0},{12,4},{16,8},{20,12},{24,16},{28,20},{1,25},{... | collective-permute-start | bytes 147464 | tf_op jit(solution)/shard_map/ppermute | solution.py:19
  22.0 5.9 %collective-permute-start.3 = (bf16[128,192]{0,1:T(8,128)(2,1)S(1)}, bf16[128,192]{0,1:T(8,128)(2,1)S(1)}, u32[]{:S(2)}, u32[]{:S(2)}) collective-permute-start(bf16[128,192]{0,1:T(8,128)(2,1)S(1)} %get-tuple-element.104), channel_id=1, source_target_pairs={{0,8},{4,12},{8,16},{12,20},{16,24},{20,28},{24,0},{28,4},{1,9},{5... | collective-permute-start | bytes 147464 | tf_op jit(solution)/shard_map/ppermute | solution.py:19
  23.0 5.8 %collective-permute-start.4 = (bf16[128,192]{0,1:T(8,128)(2,1)S(1)}, bf16[128,192]{0,1:T(8,128)(2,1)S(1)}, u32[]{:S(2)}, u32[]{:S(2)}) collective-permute-start(bf16[128,192]{0,1:T(8,128)(2,1)S(1)} %get-tuple-element.104), channel_id=1, source_target_pairs={{0,20},{4,24},{8,28},{12,0},{16,4},{20,8},{24,12},{28,16},{1,21},{... | collective-permute-start | bytes 147464 | tf_op jit(solution)/shard_map/ppermute | solution.py:19
  26.6 6.2 %collective-permute-start.5 = (bf16[128,192]{0,1:T(8,128)(2,1)S(1)}, bf16[128,192]{0,1:T(8,128)(2,1)S(1)}, u32[]{:S(2)}, u32[]{:S(2)}) collective-permute-start(bf16[128,192]{0,1:T(8,128)(2,1)S(1)} %get-tuple-element.104), channel_id=1, source_target_pairs={{0,12},{4,16},{8,20},{12,24},{16,28},{20,0},{24,4},{28,8},{1,13},{... | collective-permute-start | bytes 147464 | tf_op jit(solution)/shard_map/ppermute | solution.py:19
  64.8 0.7 copy-start.4
where the time goes:
time: 91.7 us; the launch traced here: 91.2 us
  blocking collectives  40.2 us (44%)
  other arithmetic  16.6 us (18%)
  local copies, waits for them, and re-layouts  11.5 us (13%)
  starting transfers between devices  9.92 us (11%)
  waiting for transfers between devices  6.05 us (7%)
  between operations  4.42 us (5%)
  matrix products  2.21 us (2%)
    psum x1, blocking collectives, on_device(): loss_total = lax.psum(loss_part, 'frames')  20.8 us
    reduce_sum x16, other arithmetic, one_block(): jnp.sum(jnp.where(hits, sims_part[:, which, None, :], jnp.float32(0.0)),...  13.4 us
    psum x1, blocking collectives, on_device(): inner_products, context_squared = lax.psum((inner_products, ctx_part), 'mp')  11 us
    ppermute x6, starting transfers between devices, from_behind(): return lax.ppermute(value, axis, pairs)  9.92 us
    psum x1, blocking collectives, on_device(): norm_sq = lax.psum(jnp.sum(target * target, axis=1), 'mp')  8.39 us
    ppermute x6, waiting for transfers between devices, from_behind(): return lax.ppermute(value, axis, pairs)  6.05 us
    unnamed x21, local copies, waits for them, and re-layouts  5.12 us
    dynamic_slice x48, local copies, waits for them, and re-layouts, select_columns(): lax.map(one_block, (sims_blocks, slot_blocks, row_blocks))  3.6 us
  transfers between devices with their start and end apart: 6, of which 4 were waited for; matrix products, arithmetic and copies ran while one was open for 0% of the time, Pallas kernels for 0%

commit v1 on v0

v1 whole, which is shorter than its diff:
```python
import functools

import jax
import jax.numpy as jnp
from jax import lax
from jax.experimental import pallas as pl
from jax.experimental.pallas import tpu as pltpu
from jax.sharding import PartitionSpec as P

V = 320
G = 2
REACH = 3

gumbel_softness = 2.0
logit_softness = 0.1
norm_epsilon = 1e-06

MESH = pl.DeviceIdType.MESH
OFFSETS = tuple(s * o for o in range(1, REACH + 1) for s in (1, -1))
LANES = 128


def group_softmax(values, first):
    low = jnp.float32(-jnp.inf)
    top = jnp.where(
        first,
        jnp.max(jnp.where(first, values, low), axis=1, keepdims=True),
        jnp.max(jnp.where(first, low, values), axis=1, keepdims=True),
    )
    expd = jnp.exp(values - top)
    sum0 = jnp.sum(jnp.where(first, expd, 0.0), axis=1, keepdims=True)
    sum1 = jnp.sum(jnp.where(first, 0.0, expd), axis=1, keepdims=True)
    return expd * jnp.where(first, 1.0 / sum0, 1.0 / sum1)


def kernel(
    shards, parts,
    feat_h, lw_h, gum_h, cb_h, pwt_h, ctxt_h, dist_h, mask_h,
    scores_o, loss_o, div_o,
    feat, lw, gum, cb, pwt, ctxt, dist, mask, load_sem,
    own_t, nb, t_send, t_recv,
    use_all, u_send, u_recv,
    dots_all, d_send, d_recv,
    rows_all, r_send, r_recv,
    ce_all, c_send, c_recv,
):
    own = lax.axis_index("frames")
    part = lax.axis_index("mp")
    count = feat.shape[0]
    neg = dist.shape[0]
    wide = lw.shape[1]

    loads = []
    order = ((feat_h, feat), (lw_h, lw), (gum_h, gum), (cb_h, cb), (pwt_h, pwt), (ctxt_h, ctxt), (dist_h, dist), (mask_h, mask))
    for i, (src, dst) in enumerate(order):
        load = pltpu.make_async_copy(src, dst, load_sem.at[i])
        load.start()
        loads.append(load)

    barrier = pltpu.get_barrier_semaphore()
    for o in range(1, shards):
        pl.semaphore_signal(barrier, inc=1, device_id=(lax.rem(own + o, shards), part), device_id_type=MESH)
    for o in range(1, parts):
        pl.semaphore_signal(barrier, inc=1, device_id=(own, lax.rem(part + o, parts)), device_id_type=MESH)

    loads[0].wait()
    loads[1].wait()
    logits = jnp.dot(feat[...], lw[...], preferred_element_type=jnp.float32)
    first = lax.broadcasted_iota(jnp.int32, (count, wide), 1) < V
    loads[2].wait()
    soft = group_softmax((logits + gum[...]) / gumbel_softness, first)
    loads[3].wait()
    inner = V // LANES * LANES
    outer = -(-V // LANES) * LANES
    piece0 = jnp.dot(
        jnp.where(first, soft, 0.0)[:, :outer].astype(jnp.bfloat16), cb[:outer, :],
        preferred_element_type=jnp.float32,
    ).astype(jnp.bfloat16)
    piece1 = jnp.dot(
        jnp.where(first, 0.0, soft)[:, inner:].astype(jnp.bfloat16), cb[inner:, :],
        preferred_element_type=jnp.float32,
    ).astype(jnp.bfloat16)
    codevec = jnp.concatenate([piece0, piece1], axis=1)
    loads[4].wait()
    target = lax.dot_general(
        pwt[...], codevec, (((1,), (1,)), ((), ())), preferred_element_type=jnp.float32
    )
    own_t[...] = target.astype(jnp.bfloat16)

    pl.semaphore_wait(barrier, shards - 1 + parts - 1)

    sends = []
    for j, o in enumerate(OFFSETS):
        copy = pltpu.make_async_remote_copy(
            src_ref=own_t, dst_ref=nb.at[j], send_sem=t_send.at[j], recv_sem=t_recv.at[j],
            device_id=(lax.rem(own - o + shards, shards), part), device_id_type=MESH,
        )
        copy.start()
        sends.append(copy)

    def spread_frames(buffer, send_sem, recv_sem):
        copies = []
        for o in range(1, shards):
            copy = pltpu.make_async_remote_copy(
                src_ref=buffer.at[own], dst_ref=buffer.at[own], send_sem=send_sem.at[o],
                recv_sem=recv_sem.at[own],
                device_id=(lax.rem(own + o, shards), part), device_id_type=MESH,
            )
            copy.start()
            copies.append(copy)
        return copies

    def await_frames(buffer, send_sem, recv_sem):
        for o in range(1, shards):
            source = lax.rem(own + o, shards)
            pltpu.make_async_remote_copy(
                src_ref=buffer.at[source], dst_ref=buffer.at[source], send_sem=send_sem.at[o],
                recv_sem=recv_sem.at[source],
                device_id=(source, part), device_id_type=MESH,
            ).wait_recv()

    def spread_parts(buffer, send_sem, recv_sem):
        copies = []
        for o in range(1, parts):
            copy = pltpu.make_async_remote_copy(
                src_ref=buffer.at[part], dst_ref=buffer.at[part], send_sem=send_sem.at[o],
                recv_sem=recv_sem.at[part],
                device_id=(own, lax.rem(part + o, parts)), device_id_type=MESH,
            )
            copy.start()
            copies.append(copy)
        return copies

    def await_parts(buffer, send_sem, recv_sem):
        for o in range(1, parts):
            source = lax.rem(part + o, parts)
            pltpu.make_async_remote_copy(
                src_ref=buffer.at[source], dst_ref=buffer.at[source], send_sem=send_sem.at[o],
                recv_sem=recv_sem.at[source],
                device_id=(own, source), device_id_type=MESH,
            ).wait_recv()

    clean = group_softmax(logits, first)
    use_all[own] = jnp.sum(clean, axis=0, keepdims=True)
    sends += spread_frames(use_all, u_send, u_recv)

    loads[5].wait()
    ctx_f = ctxt[...].astype(jnp.float32)
    ctx = ctx_f.T.astype(jnp.bfloat16)
    tgt_f = own_t[...].astype(jnp.float32)
    row_self = jnp.sum(ctx_f * tgt_f, axis=0, keepdims=True)
    row_norm = jnp.sum(tgt_f * tgt_f, axis=0, keepdims=True)
    row_ctx = jnp.sum(ctx_f * ctx_f, axis=0, keepdims=True)
    loads[6].wait()
    loads[7].wait()
    picks = jnp.concatenate(
        [dist[...], jnp.zeros((LANES - neg, count), jnp.int32)], axis=0
    ).astype(jnp.float32).T.astype(jnp.int32)
    owner = picks // count
    local = picks - owner * count
    distance = owner - own
    distance = jnp.where(distance < 0, distance + shards, distance)

    rows = [row_self, row_norm, row_ctx]
    dots = jnp.zeros((count, LANES), jnp.float32)
    for j, o in enumerate(OFFSETS):
        sends[j].wait_recv()
        block = nb[j]
        sims = jnp.dot(ctx, block, preferred_element_type=jnp.float32)
        block_f = block.astype(jnp.float32)
        rows.append(jnp.sum(block_f * block_f, axis=0, keepdims=True))
        taken = jnp.take_along_axis(sims, local, axis=1)
        dots = jnp.where(distance == o % shards, taken, dots)
    rows += [jnp.zeros((1, count), jnp.float32)] * (rows_all.shape[1] - len(rows))
    rows_all[part] = jnp.concatenate(rows, axis=0)
    sends += spread_parts(rows_all, r_send, r_recv)
    dots_all[part] = dots.astype(jnp.bfloat16)
    sends += spread_parts(dots_all, d_send, d_recv)

    await_parts(rows_all, r_send, r_recv)
    rows_sum = rows_all[0]
    for p in range(1, parts):
        rows_sum = rows_sum + rows_all[p]
    inverse = lax.rsqrt(rows_sum + norm_epsilon)
    scale = jnp.zeros((count, LANES), jnp.float32)
    for j, o in enumerate(OFFSETS):
        table = jnp.broadcast_to(inverse[3 + j : 4 + j], (count, LANES))
        taken = jnp.take_along_axis(table, local, axis=1)
        scale = jnp.where(distance == o % shards, taken, scale)

    await_parts(dots_all, d_send, d_recv)
    dots_sum = dots_all[0].astype(jnp.float32)
    for p in range(1, parts):
        dots_sum = dots_sum + dots_all[p].astype(jnp.float32)
    gain = inverse[2:3] / logit_softness
    others = (dots_sum * scale).T[:neg] * gain
    first_row = rows_sum[0:1] * inverse[1:2] * gain
    scores_o[0:1, :] = first_row
    scores_o[1 : neg + 1, :] = others
    total = jnp.exp(first_row) + jnp.sum(jnp.exp(others), axis=0, keepdims=True)
    cross = jnp.log(total) - first_row
    ce_all[own] = jnp.where(mask[...] == 1, cross, 0.0)
    sends += spread_frames(ce_all, c_send, c_recv)

    await_frames(use_all, u_send, u_recv)
    frames_all = count * shards
    usage = use_all[0]
    for s in range(1, shards):
        usage = usage + use_all[s]
    usage = usage / frames_all
    entropy = usage * jnp.log(usage + 1e-07)
    in_first = lax.broadcasted_iota(jnp.int32, (1, wide), 1) < V
    ent0 = jnp.sum(jnp.where(in_first, entropy, 0.0), axis=1, keepdims=True)
    ent1 = jnp.sum(jnp.where(in_first, 0.0, entropy), axis=1, keepdims=True)
    perplex = jnp.exp(-ent0) + jnp.exp(-ent1)
    div_o[0] = jnp.sum((wide - perplex) / wide)

    await_frames(ce_all, c_send, c_recv)
    losses = ce_all[0]
    for s in range(1, shards):
        losses = losses + ce_all[s]
    loss_o[0] = jnp.sum(losses) / frames_all
    for copy in sends:
        copy.wait_send()


def on_device(shards, parts, features, logit_weight, gumbel, codebook, project_weight, context, distractors, masked):
    count, neg = distractors.shape
    width = context.shape[1]
    wide = logit_weight.shape[1]
    bf16, f32 = jnp.bfloat16, jnp.float32
    operands = (
        features, logit_weight, gumbel, codebook, project_weight.T, context.T, distractors.T,
        masked.reshape(1, count),
    )
    dma = pltpu.SemaphoreType.DMA
    scores, loss, diversity = pl.pallas_call(
        functools.partial(kernel, shards, parts),
        out_shape=(
            jax.ShapeDtypeStruct((neg + 1, count), f32),
            jax.ShapeDtypeStruct((1,), f32),
            jax.ShapeDtypeStruct((1,), f32),
        ),
        in_specs=[pl.BlockSpec(memory_space=pl.ANY)] * len(operands),
        out_specs=(
            pl.BlockSpec(memory_space=pltpu.VMEM),
            pl.BlockSpec(memory_space=pltpu.SMEM),
            pl.BlockSpec(memory_space=pltpu.SMEM),
        ),
        scratch_shapes=[pltpu.VMEM(x.shape, x.dtype) for x in operands]
        + [
            dma((len(operands),)),
            pltpu.VMEM((width, count), bf16),
            pltpu.VMEM((2 * REACH, width, count), bf16), dma((2 * REACH,)), dma((2 * REACH,)),
            pltpu.VMEM((shards, 1, wide), f32), dma((shards,)), dma((shards,)),
            pltpu.VMEM((parts, count, LANES), bf16), dma((parts,)), dma((parts,)),
            pltpu.VMEM((parts, 16, count), f32), dma((parts,)), dma((parts,)),
            pltpu.VMEM((shards, 1, count), f32), dma((shards,)), dma((shards,)),
        ],
        compiler_params=pltpu.CompilerParams(collective_id=0, has_side_effects=True),
    )(*operands)
    return scores.T, loss.reshape(()), diversity.reshape(())


def solution(mesh):
    return jax.shard_map(
        functools.partial(on_device, mesh.shape["frames"], mesh.shape["mp"]),
        mesh=mesh,
        in_specs=(
            P("frames", None),
            P(),
            P("frames", None),
            P(),
            P(None, "mp"),
            P("frames", "mp"),
            P("frames", None),
            P("frames"),
        ),
        out_specs=(P("frames", None), P(), P()),
        check_vma=False,
    )
```

time: 91.7 us -> 29.2 us (0.32)
  blocking collectives: 40.2 us -> 0 us
  Pallas kernels: 0 us -> 23.5 us
  other arithmetic: 16.6 us -> 0 us
  local copies, waits for them, and re-layouts: 11.5 us -> 1.43 us
  starting transfers between devices: 9.92 us -> 0 us
  waiting for transfers between devices: 6.05 us -> 0 us
  matrix products: 2.21 us -> 0 us
    psum x3 -> x0, blocking collectives: 40.2 us -> none  [the longest x1 20.8 us: on_device(): loss_total = lax.psum(loss_part, 'frames')]
    pallas_call x0 -> x1, Pallas kernels: none -> 23.5 us  [on_device(): pl.pallas_call(functools.partial(kernel, shards, parts), out_shape=(jax.S...]
    reduce_sum x22 -> x0, other arithmetic: 15.1 us -> none  [the longest x16 13.4 us: one_block(): jnp.sum(jnp.where(hits, sims_part[:, which, None, :], jnp.float32(0.0)),...]
    ppermute x6 -> x0, starting transfers between devices: 9.92 us -> none  [from_behind(): return lax.ppermute(value, axis, pairs)]
    ppermute x6 -> x0, waiting for transfers between devices: 6.05 us -> none  [from_behind(): return lax.ppermute(value, axis, pairs)]
    unnamed x21 -> x1, local copies, waits for them, and re-layouts: 5.12 us -> 1.43 us
    dynamic_slice x48 -> x0, local copies, waits for them, and re-layouts: 3.6 us -> none  [select_columns(): lax.map(one_block, (sims_blocks, slot_blocks, row_blocks))]
    dot_general x5 -> x0, matrix products: 2.21 us -> none  [the longest x1 1.17 us: on_device(): jnp.dot(features, logit_weight, preferred_element_type=jnp.float32)]
  transfers between devices with their start and end apart: 6 -> 0, of which waited for: 4 -> 0; matrix products, arithmetic and copies ran while one was open for 0% -> 0% of each run, Pallas kernels for 0% -> 0%
where the time goes in v1:
time: 29.2 us; the launch traced here: 29 us
  Pallas kernels  23.5 us (80%)
  between operations  4.08 us (14%)
  local copies, waits for them, and re-layouts  1.43 us (5%)
    pallas_call x1, Pallas kernels, on_device(): pl.pallas_call(functools.partial(kernel, shards, parts), out_shape=(jax.S...  23.5 us
    unnamed x1, local copies, waits for them, and re-layouts  1.43 us

profile of v1, /device:TPU:0, one launch (start us, length us, event | category | flops | bytes accessed | tf_op | source)
XLA Modules:
  0.0 29.0 jit_solution(1317638777920558654)
XLA Ops:
  0.6 23.5 %shard_map.103 = (f32[101,128]{1,0:T(8,128)}, f32[1]{0:T(128)}, f32[1]{0:T(128)}) custom-call(bf16[128,512]{1,0:T(8,128)(2,1)} %feat_h.1, bf16[512,640]{1,0:T(8,128)(2,1)} %lw_h.1, f32[128,640]{1,0:T(8,128)} %gum_h.1, bf16[640,384]{1,0:T(8,128)(2,1)} %cb_h.1, bf16[192,768]{1,0:T(8,128)(2,1)} %bitcast.7, bf16[192,128]{1,0:T(8,128)(2,1)} %bitcast.10, ...), custom_call_target="tpu_custom_call" | custom-call | tf_op jit(solution)/shard_map/pallas_call | solution.py:237
  24.1 1.4 %copy.14 = f32[128,101]{0,1:T(8,128)} copy(f32[128,101]{0,1:T(8,128)} %bitcast.8) | data formatting | bytes 103424

commit v2 on v1

--- a/solution.py
+++ b/solution.py
@@ -16,7 +16,6 @@
 norm_epsilon = 1e-06
 
 MESH = pl.DeviceIdType.MESH
-OFFSETS = tuple(s * o for o in range(1, REACH + 1) for s in (1, -1))
 LANES = 128
 
 
@@ -89,14 +88,22 @@
 
     pl.semaphore_wait(barrier, shards - 1 + parts - 1)
 
-    sends = []
-    for j, o in enumerate(OFFSETS):
+    pair = 1 - 2 * lax.rem(own, 2)
+    offsets = (pair, 2, -2, 2 + pair, pair - 2, -3 * pair)
+    steps = (pair, -2, 2, pair - 2, pair + 2, -3 * pair)
+    distances = [lax.rem(o + shards, shards) for o in offsets]
+
+    def hand(src, j, step):
         copy = pltpu.make_async_remote_copy(
-            src_ref=own_t, dst_ref=nb.at[j], send_sem=t_send.at[j], recv_sem=t_recv.at[j],
-            device_id=(lax.rem(own - o + shards, shards), part), device_id_type=MESH,
+            src_ref=src, dst_ref=nb.at[j], send_sem=t_send.at[j], recv_sem=t_recv.at[j],
+            device_id=(lax.rem(own + step + shards, shards), part), device_id_type=MESH,
         )
         copy.start()
-        sends.append(copy)
+        return copy
+
+    route = (5, 4, 3, 2, 1, 0)
+    arrivals = {j: hand(own_t, j, steps[j]) for j in route}
+    sends = list(arrivals.values())
 
     def spread_frames(buffer, send_sem, recv_sem):
         copies = []
@@ -142,7 +149,6 @@
 
     clean = group_softmax(logits, first)
     use_all[own] = jnp.sum(clean, axis=0, keepdims=True)
-    sends += spread_frames(use_all, u_send, u_recv)
 
     loads[5].wait()
     ctx_f = ctxt[...].astype(jnp.float32)
@@ -154,28 +160,32 @@
     loads[6].wait()
     loads[7].wait()
     picks = jnp.concatenate(
-        [dist[...], jnp.zeros((LANES - neg, count), jnp.int32)], axis=0
+        [jnp.zeros((1, count), jnp.int32), dist[...], jnp.zeros((LANES - neg - 1, count), jnp.int32)], axis=0
     ).astype(jnp.float32).T.astype(jnp.int32)
     owner = picks // count
     local = picks - owner * count
     distance = owner - own
     distance = jnp.where(distance < 0, distance + shards, distance)
 
-    rows = [row_self, row_norm, row_ctx]
+    norms = [None] * len(offsets)
     dots = jnp.zeros((count, LANES), jnp.float32)
-    for j, o in enumerate(OFFSETS):
-        sends[j].wait_recv()
+    last = 0
+    for j in (2, 1, 5, 4, 3, last):
+        arrivals[j].wait_recv()
         block = nb[j]
+        block_f = block.astype(jnp.float32)
+        norms[j] = jnp.sum(block_f * block_f, axis=0, keepdims=True)
+        if j == last:
+            rows = [row_self, row_norm, row_ctx] + norms
+            rows += [jnp.zeros((1, count), jnp.float32)] * (rows_all.shape[1] - len(rows))
+            rows_all[part] = jnp.concatenate(rows, axis=0)
+            sends += spread_parts(rows_all, r_send, r_recv)
         sims = jnp.dot(ctx, block, preferred_element_type=jnp.float32)
-        block_f = block.astype(jnp.float32)
-        rows.append(jnp.sum(block_f * block_f, axis=0, keepdims=True))
         taken = jnp.take_along_axis(sims, local, axis=1)
-        dots = jnp.where(distance == o % shards, taken, dots)
-    rows += [jnp.zeros((1, count), jnp.float32)] * (rows_all.shape[1] - len(rows))
-    rows_all[part] = jnp.concatenate(rows, axis=0)
-    sends += spread_parts(rows_all, r_send, r_recv)
+        dots = jnp.where(distance == distances[j], taken, dots)
     dots_all[part] = dots.astype(jnp.bfloat16)
     sends += spread_parts(dots_all, d_send, d_recv)
+    sends += spread_frames(use_all, u_send, u_recv)
 
     await_parts(rows_all, r_send, r_recv)
     rows_sum = rows_all[0]
@@ -183,21 +193,21 @@
         rows_sum = rows_sum + rows_all[p]
     inverse = lax.rsqrt(rows_sum + norm_epsilon)
     scale = jnp.zeros((count, LANES), jnp.float32)
-    for j, o in enumerate(OFFSETS):
+    for j, d in enumerate(distances):
         table = jnp.broadcast_to(inverse[3 + j : 4 + j], (count, LANES))
         taken = jnp.take_along_axis(table, local, axis=1)
-        scale = jnp.where(distance == o % shards, taken, scale)
+        scale = jnp.where(distance == d, taken, scale)
 
     await_parts(dots_all, d_send, d_recv)
     dots_sum = dots_all[0].astype(jnp.float32)
     for p in range(1, parts):
         dots_sum = dots_sum + dots_all[p].astype(jnp.float32)
     gain = inverse[2:3] / logit_softness
-    others = (dots_sum * scale).T[:neg] * gain
+    row = lax.broadcasted_iota(jnp.int32, (LANES, count), 0)
     first_row = rows_sum[0:1] * inverse[1:2] * gain
-    scores_o[0:1, :] = first_row
-    scores_o[1 : neg + 1, :] = others
-    total = jnp.exp(first_row) + jnp.sum(jnp.exp(others), axis=0, keepdims=True)
+    found = jnp.where(row == 0, first_row, (dots_sum * scale).T * gain)
+    scores_o[...] = found[: neg + 1]
+    total = jnp.sum(jnp.where(row <= neg, jnp.exp(found), 0.0), axis=0, keepdims=True)
     cross = jnp.log(total) - first_row
     ce_all[own] = jnp.where(mask[...] == 1, cross, 0.0)
     sends += spread_frames(ce_all, c_send, c_recv)
@@ -237,9 +247,9 @@
     scores, loss, diversity = pl.pallas_call(
         functools.partial(kernel, shards, parts),
         out_shape=(
-            jax.ShapeDtypeStruct((neg + 1, count), f32),
-            jax.ShapeDtypeStruct((1,), f32),
-            jax.ShapeDtypeStruct((1,), f32),
+            pltpu.VMEM((neg + 1, count), f32),
+            pltpu.SMEM((1,), f32),
+            pltpu.SMEM((1,), f32),
         ),
         in_specs=[pl.BlockSpec(memory_space=pl.ANY)] * len(operands),
         out_specs=(

time: 29.2 us -> 25.4 us (0.87)
  between operations: 4.08 us -> 1.68 us
  local copies, waits for them, and re-layouts: 1.43 us -> 0.62 us
  Pallas kernels: 23.5 us -> 22.9 us
    unnamed x1, local copies, waits for them, and re-layouts: 1.43 us -> 0.62 us
    pallas_call x1, Pallas kernels: 23.5 us -> 22.9 us  [on_device(): pl.pallas_call(functools.partial(kernel, shards, parts), out_shape=(pltpu...]
where the time goes in v2:
time: 25.4 us; the launch traced here: 25.2 us
  Pallas kernels  22.9 us (90%)
  between operations  1.68 us (7%)
  local copies, waits for them, and re-layouts  0.62 us (2%)
    pallas_call x1, Pallas kernels, on_device(): pl.pallas_call(functools.partial(kernel, shards, parts), out_shape=(pltpu...  22.9 us
    unnamed x1, local copies, waits for them, and re-layouts  0.62 us

profile of v2, /device:TPU:0, one launch (start us, length us, event | category | flops | bytes accessed | tf_op | source)
XLA Modules:
  0.0 25.2 jit_solution(14711145975482893420)
XLA Ops:
  0.6 22.9 %shard_map.103 = (f32[101,128]{1,0:T(8,128)S(1)}, f32[1]{0:T(128)S(4)}, f32[1]{0:T(128)S(4)}) custom-call(bf16[128,512]{1,0:T(8,128)(2,1)} %feat_h.1, bf16[512,640]{1,0:T(8,128)(2,1)} %lw_h.1, f32[128,640]{1,0:T(8,128)} %gum_h.1, bf16[640,384]{1,0:T(8,128)(2,1)} %cb_h.1, bf16[192,768]{1,0:T(8,128)(2,1)} %bitcast.8, bf16[192,128]{1,0:T(8,128)(2,1)} %bitcast.10, ...), custom_call_target="tpu_custom_call" | custom-call | tf_op jit(solution)/shard_map/pallas_call | solution.py:247
  24.6 0.6 %copy.14 = f32[128,101]{0,1:T(8,128)} copy(f32[128,101]{0,1:T(8,128)S(1)} %bitcast.7) | data formatting | bytes 103424

commit v3 on v2

--- a/solution.py
+++ b/solution.py
@@ -35,7 +35,7 @@
 def kernel(
     shards, parts,
     feat_h, lw_h, gum_h, cb_h, pwt_h, ctxt_h, dist_h, mask_h,
-    scores_o, loss_o, div_o,
+    scores_o, pair_o,
     feat, lw, gum, cb, pwt, ctxt, dist, mask, load_sem,
     own_t, nb, t_send, t_recv,
     use_all, u_send, u_recv,
@@ -223,13 +223,13 @@
     ent0 = jnp.sum(jnp.where(in_first, entropy, 0.0), axis=1, keepdims=True)
     ent1 = jnp.sum(jnp.where(in_first, 0.0, entropy), axis=1, keepdims=True)
     perplex = jnp.exp(-ent0) + jnp.exp(-ent1)
-    div_o[0] = jnp.sum((wide - perplex) / wide)
+    pair_o[1] = jnp.sum((wide - perplex) / wide)
 
     await_frames(ce_all, c_send, c_recv)
     losses = ce_all[0]
     for s in range(1, shards):
         losses = losses + ce_all[s]
-    loss_o[0] = jnp.sum(losses) / frames_all
+    pair_o[0] = jnp.sum(losses) / frames_all
     for copy in sends:
         copy.wait_send()
 
@@ -244,17 +244,15 @@
         masked.reshape(1, count),
     )
     dma = pltpu.SemaphoreType.DMA
-    scores, loss, diversity = pl.pallas_call(
+    scores, both = pl.pallas_call(
         functools.partial(kernel, shards, parts),
         out_shape=(
             pltpu.VMEM((neg + 1, count), f32),
-            pltpu.SMEM((1,), f32),
-            pltpu.SMEM((1,), f32),
+            pltpu.SMEM((2,), f32),
         ),
         in_specs=[pl.BlockSpec(memory_space=pl.ANY)] * len(operands),
         out_specs=(
             pl.BlockSpec(memory_space=pltpu.VMEM),
-            pl.BlockSpec(memory_space=pltpu.SMEM),
             pl.BlockSpec(memory_space=pltpu.SMEM),
         ),
         scratch_shapes=[pltpu.VMEM(x.shape, x.dtype) for x in operands]
@@ -269,7 +267,7 @@
         ],
         compiler_params=pltpu.CompilerParams(collective_id=0, has_side_effects=True),
     )(*operands)
-    return scores.T, loss.reshape(()), diversity.reshape(())
+    return scores.T, both[0], both[1]
 
 
 def solution(mesh):

time: 25.4 us -> 25 us (0.984)
  between operations: 1.68 us -> 0.64 us
  local copies, waits for them, and re-layouts: 0.62 us -> 1.23 us
    slice x0 -> x1, local copies, waits for them, and re-layouts: none -> 0.6 us  [on_device(): return (scores.T, both[0], both[1])]
where the time goes in v3:
time: 25 us; the launch traced here: 24.8 us
  Pallas kernels  22.9 us (92%)
  local copies, waits for them, and re-layouts  1.23 us (5%)
  between operations  0.64 us (3%)
    pallas_call x1, Pallas kernels, on_device(): pl.pallas_call(functools.partial(kernel, shards, parts), out_shape=(pltpu...  22.9 us
    unnamed x1, local copies, waits for them, and re-layouts  0.62 us
    slice x1, local copies, waits for them, and re-layouts, on_device(): return (scores.T, both[0], both[1])  0.6 us

profile of v3, /device:TPU:0, one launch (start us, length us, event | category | flops | bytes accessed | tf_op | source)
XLA Modules:
  0.0 24.8 jit_solution(5097862777469410487)
XLA Ops:
  0.6 22.9 %shard_map.103 = (f32[101,128]{1,0:T(8,128)S(1)}, f32[2]{0:T(128)S(4)}) custom-call(bf16[128,512]{1,0:T(8,128)(2,1)} %feat_h.1, bf16[512,640]{1,0:T(8,128)(2,1)} %lw_h.1, f32[128,640]{1,0:T(8,128)} %gum_h.1, bf16[640,384]{1,0:T(8,128)(2,1)} %cb_h.1, bf16[192,768]{1,0:T(8,128)(2,1)} %bitcast.8, bf16[192,128]{1,0:T(8,128)(2,1)} %bitcast.10, ...), custom_call_target="tpu_custom_call" | custom-call | tf_op jit(solution)/shard_map/pallas_call | solution.py:247
  23.6 0.6 %copy.12 = f32[128,101]{0,1:T(8,128)} copy(f32[128,101]{0,1:T(8,128)S(1)} %bitcast.7) | data formatting | bytes 103424
  24.2 0.6 %fusion = (f32[1]{0:T(128)}, f32[1]{0:T(128)}) fusion(f32[2]{0:T(128)S(4)} %get-tuple-element.6), kind=kLoop, calls=%fused_computation | loop fusion | bytes 16 | tf_op jit(solution)/shard_map/slice | solution.py:270
